TPU v7x, 256 devices: a whole 4x4x8 slice. The times are simulated.
256 devices in a mesh: expert: 64 (over z, x, core), tensor: 4 (over y).
Axes of the slice: x: 4, y: 4, z: 8, core: 2. Of those that a mesh axis runs over, the one named last changes fastest.
Arguments:
- tokens: bfloat16 [2048, 4096], P('expert', 'tensor'), may hold values from -6 to 6
- cotangent: bfloat16 [2048, 4096], P('expert', 'tensor'), may hold values from -6 to 6
- routing: int32 [2048, 8], P('expert'), may hold values from 0 to 63, as said below
- gates: float32 [2048, 8], P('expert'), may hold values from 0.1 to 0.4
- w_in: bfloat16 [64, 4096, 1536], P('expert', None, 'tensor'), may hold values from -0.09375 to 0.09375
- w_out: bfloat16 [64, 1536, 4096], P('expert', 'tensor'), may hold values from -0.15625 to 0.15625
Outputs:
- mixed: bfloat16 [2048, 4096], P('expert', 'tensor')
- d_tokens: bfloat16 [2048, 4096], P('expert', 'tensor')
- d_w_in: bfloat16 [64, 4096, 1536], P('expert', None, 'tensor')
- d_w_out: bfloat16 [64, 1536, 4096], P('expert', 'tensor')
Inputs may be any that keep to these rules, and one draw needn't show every extreme that they name: `routing`: each row names 8 different experts. In each aligned block of 32 rows (the tokens of one index of the expert axis) no expert is named by more than 8 rows, and one expert is named by exactly 8 rows of every block.
All inputs are finite; a program needn't handle non-finite values.
Results may differ from a plain program's by a relative error of at most 0.0058.
Values may be sent and summed in bfloat16 or wider, within the bound.
A program may use at most 128 MiB of HBM per device.

v0:
```python
import jax
import jax.numpy as jnp
from jax import lax
from jax.sharding import PartitionSpec as P


def shards(tokens, cotangent, routing, gates, w_in, w_out):
    devices = lax.axis_size("expert")
    local_experts = w_in.shape[0]
    experts = devices * local_experts
    tok_rows = routing.shape[0]
    capacity = tok_rows // 4
    buffer_rows = experts * capacity
    highest = lax.Precision.HIGHEST
    matches = (routing[:, :, None] == jnp.arange(experts, dtype=jnp.int32)[None, None, :]).astype(
        jnp.int32
    )
    per_token = jnp.sum(matches, axis=1)
    earlier = jnp.cumsum(per_token, axis=0) - per_token
    destination = routing * capacity + jnp.take_along_axis(earlier, routing, axis=1)
    placed = (
        destination[:, :, None] == jnp.arange(buffer_rows, dtype=jnp.int32)[None, None, :]
    ).astype(jnp.float32)
    membership = jnp.sum(placed, axis=1)
    weighting = jnp.sum(placed * gates[:, :, None], axis=1)
    whole_tokens, whole_cot = (
        lax.all_gather(tokens, "tensor", axis=1, tiled=True),
        lax.all_gather(cotangent, "tensor", axis=1, tiled=True),
    )
    width = whole_tokens.shape[1]
    rows = jnp.einsum(
        "tr,td->rd",
        membership.astype(jnp.bfloat16),
        whole_tokens,
        preferred_element_type=jnp.float32,
    ).astype(jnp.bfloat16)
    scaled = jnp.einsum(
        "tr,td->rd", weighting, whole_cot.astype(jnp.float32), precision=highest
    ).astype(jnp.bfloat16)
    send_rows = rows.reshape(devices, local_experts, capacity, width)
    send_scaled = scaled.reshape(devices, local_experts, capacity, width)
    expert_rows, expert_scaled = (
        lax.all_to_all(send_rows, "expert", split_axis=0, concat_axis=0, tiled=True),
        lax.all_to_all(send_scaled, "expert", split_axis=0, concat_axis=0, tiled=True),
    )
    preact = jnp.einsum("nesd,edh->nesh", expert_rows, w_in, preferred_element_type=jnp.float32)
    sigmoid_val = jax.nn.sigmoid(preact)
    hidden = (preact * sigmoid_val).astype(jnp.bfloat16)
    out_part = jnp.einsum("nesh,ehd->nesd", hidden, w_out, preferred_element_type=jnp.float32)
    grad_hidden = jnp.einsum(
        "nesd,ehd->nesh", expert_scaled, w_out, preferred_element_type=jnp.float32
    )
    grad_preact = (grad_hidden * sigmoid_val * (1.0 + preact * (1.0 - sigmoid_val))).astype(
        jnp.bfloat16
    )
    d_w_out = jnp.einsum(
        "nesh,nesd->ehd", hidden, expert_scaled, preferred_element_type=jnp.float32
    ).astype(jnp.bfloat16)
    d_w_in = jnp.einsum(
        "nesd,nesh->edh", expert_rows, grad_preact, preferred_element_type=jnp.float32
    ).astype(jnp.bfloat16)
    grad_part = jnp.einsum("nesh,edh->nesd", grad_preact, w_in, preferred_element_type=jnp.float32)
    out_sums, grad_sums = (
        lax.psum_scatter(out_part, "tensor", scatter_dimension=3, tiled=True),
        lax.psum_scatter(grad_part, "tensor", scatter_dimension=3, tiled=True),
    )
    back_out, back_grad = (
        lax.all_to_all(out_sums, "expert", split_axis=0, concat_axis=0, tiled=True),
        lax.all_to_all(grad_sums, "expert", split_axis=0, concat_axis=0, tiled=True),
    )
    width_q = back_out.shape[3]
    mixed = jnp.einsum(
        "tr,rd->td", weighting, back_out.reshape(buffer_rows, width_q), precision=highest
    ).astype(jnp.bfloat16)
    d_tokens = jnp.einsum(
        "tr,rd->td", membership, back_grad.reshape(buffer_rows, width_q), precision=highest
    ).astype(jnp.bfloat16)
    return (mixed, d_tokens, d_w_in, d_w_out)


def solution(mesh):
    placed = (
        P("expert", "tensor"),
        P("expert", "tensor"),
        P("expert", None),
        P("expert", None),
        P("expert", None, "tensor"),
        P("expert", "tensor", None),
    )
    return jax.shard_map(
        shards,
        mesh=mesh,
        in_specs=placed,
        out_specs=(
            P("expert", "tensor"),
            P("expert", "tensor"),
            P("expert", None, "tensor"),
            P("expert", "tensor", None),
        ),
        check_vma=False,
    )
```

profile of v0, /device:TPU:2, one launch (start us, length us, event | category | flops | bytes accessed | tf_op | source)
XLA Modules:
  0.0 423.1 jit_solution(5423124009950122582)
XLA Ops:
  7.2 0.8 bitcast_or_fusion
  8.1 0.8 copy.47
  9.1 0.8 copy.51
  10.0 1.9 gather_fusion
  12.2 12.8 %all_gather.6 = bf16[32,4096]{1,0:T(8,128)(2,1)S(1)} all-gather(bf16[32,1024]{1,0:T(8,128)(2,1)S(1)} %copy-done.8), channel_id=1, replica_groups=mesh['expert'=64,'tensor'=4] {'tensor'}, dimensions={1}, use_global_device_ids=true | all-gather | bytes 327680 | tf_op jit(solution)/shard_map/all_gather | solution.py:27
  25.4 1.3 fusion
  26.7 108.3 %all_to_all.20 = bf16[64,1,8,4096]{3,2,1,0:T(8,128)(2,1)S(1)} all-to-all(bf16[64,1,8,4096]{3,2,1,0:T(8,128)(2,1)S(1)} %fusion), channel_id=1, replica_groups=mesh['expert'=64,'tensor'=4] {'expert'}, dimensions={0} | all-to-all | bytes 8388608 | tf_op jit(solution)/shard_map/all_to_all | solution.py:43
  135.0 2.3 fusion.18
  137.3 0.9 copy-done.5
  138.2 5.6 %convolution_bitcast_fusion.1 = f32[64,1,8,4096]{3,2,0,1:T(8,128)} fusion(bf16[1,384,4096]{2,1,0:T(8,128)(2,1)S(1)} %copy-done, f32[64,1,8,384]{3,2,0,1:T(8,128)S(1)} %fusion.18), kind=kOutput, calls=%fused_computation.2 | convolution fusion | flops 1611595776 | bytes 12320768 | tf_op jit(solution)/shard_map/nesh,ehd->nesd/dot_general | solution.py:49
  143.9 0.8 copy-done.9
  144.6 13.1 %all_gather.7 = bf16[32,4096]{1,0:T(8,128)(2,1)S(1)} all-gather(bf16[32,1024]{1,0:T(8,128)(2,1)S(1)} %copy-done.9), channel_id=1, replica_groups=mesh['expert'=64,'tensor'=4] {'tensor'}, dimensions={1}, use_global_device_ids=true | all-gather | bytes 327680 | tf_op jit(solution)/shard_map/all_gather | solution.py:28
  157.7 3.7 fusion.1
  161.5 101.6 %all_to_all.21 = bf16[64,1,8,4096]{3,2,1,0:T(8,128)(2,1)S(1)} all-to-all(bf16[64,1,8,4096]{3,2,1,0:T(8,128)(2,1)S(1)} %fusion.1), channel_id=1, replica_groups=mesh['expert'=64,'tensor'=4] {'expert'}, dimensions={0} | all-to-all | bytes 8388608 | tf_op jit(solution)/shard_map/all_to_all | solution.py:44
  263.1 2.4 fusion.43
  266.5 5.6 %convolution_bitcast_fusion = f32[64,1,8,4096]{3,2,0,1:T(8,128)} fusion(bf16[64,8,384]{2,1,0:T(8,128)(2,1)S(1)} %fusion.43, bf16[1,4096,384]{2,1,0:T(8,128)(2,1)S(1)} %copy-done.4), kind=kOutput, calls=%fused_computation.1 | convolution fusion | flops 1610612736 | bytes 11927552 | tf_op jit(solution)/shard_map/nesh,edh->nesd/dot_general | solution.py:62
  272.1 5.6 %all-to-all-start.1 = ((f32[64,1,8,1024]{3,2,1,0:T(8,128)}), f32[64,1,8,1024]{3,2,1,0:T(8,128)}, u32[]{:S(2)}, u32[]{:S(2)}) async-start(f32[64,1,8,1024]{3,2,1,0:T(8,128)} %bitcast.128), calls=%async_computation.2 | async-start | bytes 4194304 | tf_op jit(solution)/shard_map/all_to_all | solution.py:68
  277.8 6.8 %fusion.3 = bf16[1,384,4096]{2,1,0:T(8,128)(2,1)} fusion(bf16[64,1,8,4096]{3,2,1,0:T(8,128)(2,1)} %copy-done.2, f32[64,1,8,384]{3,2,0,1:T(8,128)} %copy-done.5), kind=kOutput, calls=%fused_computation.10 | convolution fusion | flops 1613168640 | bytes 8126464 | tf_op jit(solution)/shard_map/nesh,nesd->ehd/dot_general | solution.py:56
  284.5 66.3 %reduce-scatter.5.cloned.1.call-done = f32[64,1,8,1024]{3,2,0,1:T(8,128)} async-done(((f32[64,1,8,4096]{3,2,0,1:T(8,128)}), f32[64,1,8,1024]{3,2,0,1:T(8,128)}) %reduce-scatter.5.cloned.1.call-update) | async-done | bytes 2097168 | tf_op jit(solution)/shard_map/reduce_scatter | solution.py:65
  350.9 10.7 %all-to-all-start.3 = ((f32[64,1,8,1024]{3,2,1,0:T(8,128)}), f32[64,1,8,1024]{3,2,1,0:T(8,128)}, u32[]{:S(2)}, u32[]{:S(2)}) async-start(f32[64,1,8,1024]{3,2,1,0:T(8,128)} %bitcast.129), calls=%async_computation.5 | async-start | bytes 4194304 | tf_op jit(solution)/shard_map/all_to_all | solution.py:69
  361.6 6.3 %fusion.2 = bf16[1,4096,384]{2,1,0:T(8,128)(2,1)} fusion(bf16[64,8,384]{2,1,0:T(8,128)(2,1)} %copy-done.7, bf16[64,1,8,4096]{3,2,1,0:T(8,128)(2,1)} %copy-done.1), kind=kOutput, calls=%fused_computation.9 | convolution fusion | flops 1612185600 | bytes 7733248 | tf_op jit(solution)/shard_map/nesd,nesh->edh/dot_general | solution.py:59
  367.9 3.5 fusion.48
  371.4 41.3 %all-to-all-done.3 = f32[64,1,8,1024]{3,2,1,0:T(8,128)} async-done(((f32[64,1,8,1024]{3,2,1,0:T(8,128)}), f32[64,1,8,1024]{3,2,1,0:T(8,128)}, u32[]{:S(2)}, u32[]{:S(2)}) %all-to-all-start.3) | async-done | bytes 2097184 | tf_op jit(solution)/shard_map/all_to_all | solution.py:69
  412.8 3.5 fusion.51
  (36 shorter events, 2.1 us)
Async XLA Ops:
  7.2 131.1 %copy-start = (bf16[1,384,4096]{2,1,0:T(8,128)(2,1)S(1)}, bf16[1,384,4096]{2,1,0:T(8,128)(2,1)}, u32[]{:S(2)}) copy-start(bf16[1,384,4096]{2,1,0:T(8,128)(2,1)} %param.11) | copy-start | bytes 9437188
  7.2 264.9 %reduce-scatter.3.cloned.1.call-start = ((), (), s32[]{:S(2)}) async-start(), calls=%async_computation.6 | async-start | bytes 10485760 | tf_op jit(solution)/shard_map/reduce_scatter | solution.py:64
  10.0 2.1 copy-start.10
  10.0 2.2 copy-start.8
  26.7 108.3 %copy-start.3 = (bf16[1,4096,384]{2,1,0:T(8,128)(2,1)S(1)}, bf16[1,4096,384]{2,1,0:T(8,128)(2,1)}, u32[]{:S(2)}) copy-start(bf16[1,4096,384]{2,1,0:T(8,128)(2,1)} %param.10) | copy-start | bytes 9437188
  135.0 2.3 copy-start.1
  137.3 0.9 copy-start.5
  143.8 0.8 copy-start.9
  143.8 207.1 %reduce-scatter.5.cloned.1.call-start = ((), (), s32[]{:S(2)}) async-start(), calls=%async_computation.7 | async-start | bytes 10485760 | tf_op jit(solution)/shard_map/reduce_scatter | solution.py:65
  161.5 101.6 %copy-start.6 = (f32[64,1,8,384]{3,2,0,1:T(8,128)S(1)}, f32[64,1,8,384]{3,2,0,1:T(8,128)}, u32[]{:S(2)}) copy-start(f32[64,1,8,384]{3,2,0,1:T(8,128)} %copy-done.5) | copy-start | bytes 2359300
  263.1 2.5 copy-start.2
  263.1 3.4 copy-start.4
  265.5 0.7 copy-start.7
  272.1 78.7 %all-to-all-start.1 = ((f32[64,1,8,1024]{3,2,1,0:T(8,128)}), f32[64,1,8,1024]{3,2,1,0:T(8,128)}, u32[]{:S(2)}, u32[]{:S(2)}) async-start(f32[64,1,8,1024]{3,2,1,0:T(8,128)} %bitcast.128), calls=%async_computation.2 | async-start | bytes 4194304 | tf_op jit(solution)/shard_map/all_to_all | solution.py:68
  350.9 61.9 %all-to-all-start.3 = ((f32[64,1,8,1024]{3,2,1,0:T(8,128)}), f32[64,1,8,1024]{3,2,1,0:T(8,128)}, u32[]{:S(2)}, u32[]{:S(2)}) async-start(f32[64,1,8,1024]{3,2,1,0:T(8,128)} %bitcast.129), calls=%async_computation.5 | async-start | bytes 4194304 | tf_op jit(solution)/shard_map/all_to_all | solution.py:69
Sparse Core Ops, SparseCore 0:
  143.9 79.4 reduce-scatter.2
  272.2 78.6 reduce-scatter.4
where the time goes:
time: 424 us; the launch traced here: 423 us
  blocking collectives  236 us (56%)
  waiting for transfers between devices  108 us (25%)
  matrix products  41 us (10%)
  starting transfers between devices  16.4 us (4%)
  between operations  14.2 us (3%)
  local copies, waits for them, and re-layouts  6.55 us (2%)
    all_to_all x1, blocking collectives, shards(): lax.all_to_all(send_rows, 'expert', split_axis=0, concat_axis=0, tiled=True)  108 us
    all_to_all x1, blocking collectives, shards(): lax.all_to_all(send_scaled, 'expert', split_axis=0, concat_axis=0, tiled=...  102 us
    reduce_scatter x1, waiting for transfers between devices, shards(): lax.psum_scatter(grad_part, 'tensor', scatter_dimension=3, tiled=True)  66.3 us
    all_to_all x1, waiting for transfers between devices, shards(): lax.all_to_all(grad_sums, 'expert', split_axis=0, concat_axis=0, tiled=True)  41.3 us
    all_gather x1, blocking collectives, shards(): lax.all_gather(cotangent, 'tensor', axis=1, tiled=True)  13.1 us
    all_gather x1, blocking collectives, shards(): lax.all_gather(tokens, 'tensor', axis=1, tiled=True)  12.8 us
    all_to_all x1, starting transfers between devices, shards(): lax.all_to_all(grad_sums, 'expert', split_axis=0, concat_axis=0, tiled=True)  10.7 us
  transfers between devices with their start and end apart: 4, of which 2 were waited for; matrix products, arithmetic and copies ran while one was open for 7% of the time, Pallas kernels for 0%

commit v1 on v0

--- a/solution.py
+++ b/solution.py
@@ -24,7 +24,9 @@
     membership = jnp.sum(placed, axis=1)
     weighting = jnp.sum(placed * gates[:, :, None], axis=1)
     whole_tokens, whole_cot = (
-        lax.all_gather(tokens, "tensor", axis=1, tiled=True),
+        jnp.concatenate(
+            lax.all_to_all(jnp.stack([tokens] * lax.axis_size("tensor")), "tensor", 0, 0), axis=1
+        ),
         lax.all_gather(cotangent, "tensor", axis=1, tiled=True),
     )
     width = whole_tokens.shape[1]

time: 424 us -> 418 us (0.986)
  blocking collectives: 236 us -> 223 us
  starting transfers between devices: 16.4 us -> 20.9 us
    all_gather x1 -> x0, blocking collectives: 12.8 us -> none  [shards(): lax.all_gather(tokens, 'tensor', axis=1, tiled=True)]
    all_to_all x0 -> x1, starting transfers between devices: none -> 4.46 us  [shards(): lax.all_to_all(jnp.stack([tokens] * lax.axis_size('tensor')), 'tensor', 0...]
  transfers between devices with their start and end apart: 4 -> 5, of which waited for: 2 -> 3; matrix products, arithmetic and copies ran while one was open for 7% -> 8% of each run, Pallas kernels for 0% -> 0%
where the time goes in v1:
time: 418 us; the launch traced here: 417 us
  blocking collectives  223 us (53%)
  waiting for transfers between devices  109 us (26%)
  matrix products  40.8 us (10%)
  starting transfers between devices  20.9 us (5%)
  between operations  14.2 us (3%)
  local copies, waits for them, and re-layouts  7.54 us (2%)
    all_to_all x1, blocking collectives, shards(): lax.all_to_all(send_rows, 'expert', split_axis=0, concat_axis=0, tiled=True)  108 us
    all_to_all x1, blocking collectives, shards(): lax.all_to_all(send_scaled, 'expert', split_axis=0, concat_axis=0, tiled=...  102 us
    reduce_scatter x1, waiting for transfers between devices, shards(): lax.psum_scatter(grad_part, 'tensor', scatter_dimension=3, tiled=True)  65.7 us
    all_to_all x1, waiting for transfers between devices, shards(): lax.all_to_all(grad_sums, 'expert', split_axis=0, concat_axis=0, tiled=True)  41.3 us
    all_gather x1, blocking collectives, shards(): lax.all_gather(cotangent, 'tensor', axis=1, tiled=True)  13 us
    all_to_all x1, starting transfers between devices, shards(): lax.all_to_all(grad_sums, 'expert', split_axis=0, concat_axis=0, tiled=True)  10.7 us
  transfers between devices with their start and end apart: 5, of which 3 were waited for; matrix products, arithmetic and copies ran while one was open for 8% of the time, Pallas kernels for 0%

profile of v1, /device:TPU:2, one launch (start us, length us, event | category | flops | bytes accessed | tf_op | source)
XLA Modules:
  0.0 417.1 jit_solution(15949248251937205197)
XLA Ops:
  7.2 1.7 stack.2
  8.9 4.5 %all-to-all-start = ((bf16[4,32,1024]{2,1,0:T(8,128)(2,1)}), bf16[4,32,1024]{2,1,0:T(8,128)(2,1)S(1)}, u32[]{:S(2)}, u32[]{:S(2)}) async-start(bf16[4,32,1024]{2,1,0:T(8,128)(2,1)} %stack.2), calls=%async_computation | async-start | bytes 524288 | tf_op jit(solution)/shard_map/all_to_all | solution.py:28
  15.2 1.9 gather_fusion
  17.5 1.0 convert_reduce_fusion
  18.5 1.5 all-to-all-done
  20.1 1.3 fusion
  21.4 108.3 %all_to_all.25 = bf16[64,1,8,4096]{3,2,1,0:T(8,128)(2,1)S(1)} all-to-all(bf16[64,1,8,4096]{3,2,1,0:T(8,128)(2,1)S(1)} %fusion), channel_id=1, replica_groups=mesh['expert'=64,'tensor'=4] {'expert'}, dimensions={0} | all-to-all | bytes 8388608 | tf_op jit(solution)/shard_map/all_to_all | solution.py:45
  129.6 2.3 fusion.18
  132.0 0.9 copy-done.5
  132.9 5.6 %convolution_bitcast_fusion.1 = f32[64,1,8,4096]{3,2,0,1:T(8,128)} fusion(bf16[1,384,4096]{2,1,0:T(8,128)(2,1)S(1)} %copy-done, f32[64,1,8,384]{3,2,0,1:T(8,128)S(1)} %fusion.18), kind=kOutput, calls=%fused_computation.2 | convolution fusion | flops 1611595776 | bytes 12320768 | tf_op jit(solution)/shard_map/nesh,ehd->nesd/dot_general | solution.py:51
  138.5 0.8 copy-done.9
  139.3 13.0 %all_gather.3 = bf16[32,4096]{1,0:T(8,128)(2,1)S(1)} all-gather(bf16[32,1024]{1,0:T(8,128)(2,1)S(1)} %copy-done.9), channel_id=1, replica_groups=mesh['expert'=64,'tensor'=4] {'tensor'}, dimensions={1}, use_global_device_ids=true | all-gather | bytes 327680 | tf_op jit(solution)/shard_map/all_gather | solution.py:30
  152.3 3.7 fusion.1
  156.0 101.9 %all_to_all.26 = bf16[64,1,8,4096]{3,2,1,0:T(8,128)(2,1)S(1)} all-to-all(bf16[64,1,8,4096]{3,2,1,0:T(8,128)(2,1)S(1)} %fusion.1), channel_id=1, replica_groups=mesh['expert'=64,'tensor'=4] {'expert'}, dimensions={0} | all-to-all | bytes 8388608 | tf_op jit(solution)/shard_map/all_to_all | solution.py:46
  258.0 2.4 fusion.43
  261.4 5.6 %convolution_bitcast_fusion = f32[64,1,8,4096]{3,2,0,1:T(8,128)} fusion(bf16[64,8,384]{2,1,0:T(8,128)(2,1)S(1)} %fusion.43, bf16[1,4096,384]{2,1,0:T(8,128)(2,1)S(1)} %copy-done.4), kind=kOutput, calls=%fused_computation.1 | convolution fusion | flops 1610612736 | bytes 11927552 | tf_op jit(solution)/shard_map/nesh,edh->nesd/dot_general | solution.py:64
  267.0 5.6 %all-to-all-start.2 = ((f32[64,1,8,1024]{3,2,1,0:T(8,128)}), f32[64,1,8,1024]{3,2,1,0:T(8,128)}, u32[]{:S(2)}, u32[]{:S(2)}) async-start(f32[64,1,8,1024]{3,2,1,0:T(8,128)} %bitcast.131), calls=%async_computation.3 | async-start | bytes 4194304 | tf_op jit(solution)/shard_map/all_to_all | solution.py:70
  272.7 6.5 %fusion.3 = bf16[1,384,4096]{2,1,0:T(8,128)(2,1)} fusion(bf16[64,1,8,4096]{3,2,1,0:T(8,128)(2,1)} %copy-done.2, f32[64,1,8,384]{3,2,0,1:T(8,128)} %copy-done.5), kind=kOutput, calls=%fused_computation.10 | convolution fusion | flops 1613168640 | bytes 8126464 | tf_op jit(solution)/shard_map/nesh,nesd->ehd/dot_general | solution.py:58
  279.2 65.7 %reduce-scatter.5.cloned.1.call-done = f32[64,1,8,1024]{3,2,0,1:T(8,128)} async-done(((f32[64,1,8,4096]{3,2,0,1:T(8,128)}), f32[64,1,8,1024]{3,2,0,1:T(8,128)}) %reduce-scatter.5.cloned.1.call-update) | async-done | bytes 2097168 | tf_op jit(solution)/shard_map/reduce_scatter | solution.py:67
  344.9 10.7 %all-to-all-start.4 = ((f32[64,1,8,1024]{3,2,1,0:T(8,128)}), f32[64,1,8,1024]{3,2,1,0:T(8,128)}, u32[]{:S(2)}, u32[]{:S(2)}) async-start(f32[64,1,8,1024]{3,2,1,0:T(8,128)} %bitcast.132), calls=%async_computation.6 | async-start | bytes 4194304 | tf_op jit(solution)/shard_map/all_to_all | solution.py:71
  355.6 6.3 %fusion.2 = bf16[1,4096,384]{2,1,0:T(8,128)(2,1)} fusion(bf16[64,8,384]{2,1,0:T(8,128)(2,1)} %copy-done.8, bf16[64,1,8,4096]{3,2,1,0:T(8,128)(2,1)} %copy-done.1), kind=kOutput, calls=%fused_computation.9 | convolution fusion | flops 1612185600 | bytes 7733248 | tf_op jit(solution)/shard_map/nesd,nesh->edh/dot_general | solution.py:61
  361.9 3.5 fusion.48
  365.4 41.3 %all-to-all-done.4 = f32[64,1,8,1024]{3,2,1,0:T(8,128)} async-done(((f32[64,1,8,1024]{3,2,1,0:T(8,128)}), f32[64,1,8,1024]{3,2,1,0:T(8,128)}, u32[]{:S(2)}, u32[]{:S(2)}) %all-to-all-start.4) | async-done | bytes 2097184 | tf_op jit(solution)/shard_map/all_to_all | solution.py:71
  406.8 3.5 fusion.51
  (41 shorter events, 3.2 us)
Async XLA Ops:
  7.2 125.7 %copy-start = (bf16[1,384,4096]{2,1,0:T(8,128)(2,1)S(1)}, bf16[1,384,4096]{2,1,0:T(8,128)(2,1)}, u32[]{:S(2)}) copy-start(bf16[1,384,4096]{2,1,0:T(8,128)(2,1)} %param.11) | copy-start | bytes 9437188
  8.9 11.1 %all-to-all-start = ((bf16[4,32,1024]{2,1,0:T(8,128)(2,1)}), bf16[4,32,1024]{2,1,0:T(8,128)(2,1)S(1)}, u32[]{:S(2)}, u32[]{:S(2)}) async-start(bf16[4,32,1024]{2,1,0:T(8,128)(2,1)} %stack.2), calls=%async_computation | async-start | bytes 524288 | tf_op jit(solution)/shard_map/all_to_all | solution.py:28
  13.4 253.6 %reduce-scatter.3.cloned.1.call-start = ((), (), s32[]{:S(2)}) async-start(), calls=%async_computation.7 | async-start | bytes 10485760 | tf_op jit(solution)/shard_map/reduce_scatter | solution.py:66
  15.2 2.1 copy-start.10
  15.2 2.1 copy-start.11
  21.3 108.3 %copy-start.3 = (bf16[1,4096,384]{2,1,0:T(8,128)(2,1)S(1)}, bf16[1,4096,384]{2,1,0:T(8,128)(2,1)}, u32[]{:S(2)}) copy-start(bf16[1,4096,384]{2,1,0:T(8,128)(2,1)} %param.10) | copy-start | bytes 9437188
  129.6 2.3 copy-start.1
  132.0 0.9 copy-start.5
  138.5 0.8 copy-start.9
  138.5 13.8 %copy-start.7 = (f32[32,512]{1,0:T(8,128)S(1)}, f32[32,512]{1,0:T(8,128)}, u32[]{:S(2)}) copy-start(f32[32,512]{1,0:T(8,128)} %get-tuple-element.5) | copy-start | bytes 196612
  138.5 206.4 %reduce-scatter.5.cloned.1.call-start = ((), (), s32[]{:S(2)}) async-start(), calls=%async_computation.8 | async-start | bytes 10485760 | tf_op jit(solution)/shard_map/reduce_scatter | solution.py:67
  156.0 101.9 %copy-start.6 = (f32[64,1,8,384]{3,2,0,1:T(8,128)S(1)}, f32[64,1,8,384]{3,2,0,1:T(8,128)}, u32[]{:S(2)}) copy-start(f32[64,1,8,384]{3,2,0,1:T(8,128)} %copy-done.5) | copy-start | bytes 2359300
  258.0 2.5 copy-start.2
  258.0 3.4 copy-start.4
  260.4 0.8 copy-start.8
  267.0 77.8 %all-to-all-start.2 = ((f32[64,1,8,1024]{3,2,1,0:T(8,128)}), f32[64,1,8,1024]{3,2,1,0:T(8,128)}, u32[]{:S(2)}, u32[]{:S(2)}) async-start(f32[64,1,8,1024]{3,2,1,0:T(8,128)} %bitcast.131), calls=%async_computation.3 | async-start | bytes 4194304 | tf_op jit(solution)/shard_map/all_to_all | solution.py:70
  344.9 61.9 %all-to-all-start.4 = ((f32[64,1,8,1024]{3,2,1,0:T(8,128)}), f32[64,1,8,1024]{3,2,1,0:T(8,128)}, u32[]{:S(2)}, u32[]{:S(2)}) async-start(f32[64,1,8,1024]{3,2,1,0:T(8,128)} %bitcast.132), calls=%async_computation.6 | async-start | bytes 4194304 | tf_op jit(solution)/shard_map/all_to_all | solution.py:71
Sparse Core Ops, SparseCore 0:
  138.6 78.9 reduce-scatter.2
  267.1 77.7 reduce-scatter.4
